TPU v7x, 32 devices: a whole 2x2x4 slice. The times are simulated.
32 devices in a mesh: heads: 4 (over y, core), seq: 8 (over z, x).
Axes of the slice: x: 2, y: 2, z: 4, core: 2. Of those that a mesh axis runs over, the one named last changes fastest.
Arguments:
- queries: bfloat16 [1024, 64, 576], P('seq', 'heads'), may hold values from -6 to 6
- latents: bfloat16 [8, 128, 576], P('seq', 'heads'), may hold values from -6 to 6
- grad_out: bfloat16 [1024, 64, 512], P('seq', 'heads'), may hold values from -6 to 6
- selected: int32 [8, 4], P('seq'), may hold values from 0 to 7, as said below
Outputs:
- output: bfloat16 [1024, 64, 512], P('seq', 'heads')
- grad_query: bfloat16 [1024, 64, 576], P('seq', 'heads')
- latent_grad: float32 [8, 128, 576], P('seq', 'heads')
Inputs may be any that keep to these rules, and one draw needn't show every extreme that they name: `selected`: row i lists 4 different blocks, none of them held on the same index of seq as block i (blocks i and j share it when i // 1 equals j // 1); how often a block is chosen varies widely between blocks.
All inputs are finite; a program needn't handle non-finite values.
Results may differ from a plain program's by a relative error of at most 0.012.
Values may be sent and summed in bfloat16 or wider, within the bound.
A program may use at most 64 MiB of HBM per device.

v0:
```python
import jax
import jax.numpy as jnp
from jax import lax
from jax.sharding import PartitionSpec as P


def shards(queries, latents, grad_out, selected):
    block_count, row_share, key_width = latents.shape
    token_total, head_count, _ = queries.shape
    value_width = grad_out.shape[2]
    key_blocks = selected.shape[1] + 1
    block_size = token_total // block_count
    score_scale = key_width ** (-0.5)
    slices = lax.all_gather(latents, "seq", axis=0, tiled=True)
    list_blocks = slices.shape[0]
    own_blocks = lax.axis_index("seq") * block_count + jnp.arange(block_count, dtype=jnp.int32)
    block_ids = jnp.concatenate([own_blocks[:, None], selected], axis=1).reshape(-1)
    picked = jnp.take(slices, block_ids, axis=0)
    key_row_tiles = lax.all_gather(picked, "heads", axis=1, tiled=True)
    key_row_tiles = key_row_tiles.reshape(block_count, key_blocks * block_size, key_width)
    value_rows = key_row_tiles[:, :, :value_width]
    query_row_tiles = queries.reshape(block_count, block_size, head_count, key_width)
    grad_rows = grad_out.reshape(block_count, block_size, head_count, value_width)
    scores = (
        jnp.einsum(
            "gonv,gmv->gnom", query_row_tiles, key_row_tiles, preferred_element_type=jnp.float32
        )
        * score_scale
    )
    prob_full = jax.nn.softmax(scores, axis=-1)
    prob_half = prob_full.astype(jnp.bfloat16)
    output = jnp.einsum(
        "bhtk,bkl->bthl", prob_half, value_rows, preferred_element_type=jnp.float32
    ).astype(jnp.bfloat16)
    row_delta = jnp.sum(grad_rows.astype(jnp.float32) * output.astype(jnp.float32), axis=-1)
    grad_prob = jnp.einsum(
        "bthl,bkl->bhtk", grad_rows, value_rows, preferred_element_type=jnp.float32
    )
    score_gradient = (
        prob_full * (grad_prob - jnp.transpose(row_delta, (0, 2, 1))[..., None]) * score_scale
    ).astype(jnp.bfloat16)
    grad_query = jnp.einsum(
        "mfgv,mvq->mgfq", score_gradient, key_row_tiles, preferred_element_type=jnp.float32
    ).astype(jnp.bfloat16)
    key_gradient = jnp.einsum(
        "jxnq,jnxa->jqa", score_gradient, query_row_tiles, preferred_element_type=jnp.float32
    )
    grad_value = jnp.einsum(
        "bhtk,bthl->bkl", prob_half, grad_rows, preferred_element_type=jnp.float32
    )
    key_gradient = jnp.concatenate(
        [key_gradient[:, :, :value_width] + grad_value, key_gradient[:, :, value_width:]], axis=-1
    )
    contrib = key_gradient.reshape(block_count * key_blocks, block_size, key_width)
    head_total = lax.psum(contrib, "heads")
    own_share = lax.dynamic_slice_in_dim(
        head_total, lax.axis_index("heads") * row_share, row_share, 1
    )
    one_hot = (jnp.arange(list_blocks, dtype=jnp.int32)[:, None] == block_ids[None, :]).astype(
        jnp.float32
    )
    dense_grad = jnp.dot(
        one_hot,
        own_share.reshape(block_count * key_blocks, row_share * key_width),
        precision=lax.Precision.HIGHEST,
        preferred_element_type=jnp.float32,
    )
    dense_grad = dense_grad.reshape(list_blocks, row_share, key_width)
    holders = list_blocks // block_count
    bundles = dense_grad.reshape(1, holders * block_count, row_share, key_width)
    arrived = lax.all_to_all(bundles, "seq", split_axis=1, concat_axis=0, tiled=True)
    latent_grad = jnp.sum(arrived, axis=0)
    return (
        output.reshape(token_total, head_count, value_width),
        grad_query.reshape(token_total, head_count, key_width),
        latent_grad,
    )


def solution(mesh):
    in_specs = (
        P("seq", "heads", None),
        P("seq", "heads", None),
        P("seq", "heads", None),
        P("seq", None),
    )
    out_specs = (P("seq", "heads", None), P("seq", "heads", None), P("seq", "heads", None))
    return jax.shard_map(shards, mesh=mesh, in_specs=in_specs, out_specs=out_specs, check_vma=False)
```

profile of v0, /device:TPU:0, one launch (start us, length us, event | category | flops | bytes accessed | tf_op | source)
XLA Modules:
  0.0 150.2 jit_solution(12962128840217296627)
XLA Ops:
  7.2 0.9 compare_and_fusion
  8.1 32.9 %all_gather.6 = bf16[8,32,576]{2,1,0:T(8,128)(2,1)S(1)} all-gather(bf16[1,32,576]{2,1,0:T(8,128)(2,1)} %param.5), channel_id=1, replica_groups=mesh['heads'=4,'seq'=8] {'seq'}, dimensions={0}, use_global_device_ids=true | all-gather | bytes 331776 | tf_op jit(solution)/shard_map/all_gather | solution.py:14
  41.0 0.6 gather_fusion
  41.7 8.8 %all_gather.7 = bf16[5,128,576]{2,1,0:T(8,128)(2,1)S(1)} all-gather(bf16[5,32,576]{2,1,0:T(8,128)(2,1)S(1)} %broadcast_select_fusion), channel_id=1, replica_groups=mesh['heads'=4,'seq'=8] {'heads'}, dimensions={1}, use_global_device_ids=true | all-gather | bytes 921600 | tf_op jit(solution)/shard_map/all_gather | solution.py:19
  50.5 4.8 %copy.37 = bf16[128,16,512]{0,2,1:T(8,128)(2,1)} copy(bf16[128,16,512]{2,1,0:T(8,128)(2,1)} %param.6) | data formatting | bytes 4194304 | tf_op args[2]
  55.3 2.2 %bitcast_reduce_fusion = (f32[16,128]{1,0:T(8,128)S(1)}, f32[640,128,16]{1,0,2:T(8,128)S(1)}) fusion(bf16[640,576,1]{1,0,2:T(8,128)(2,1)S(1)} %bitcast.124, bf16[128,16,576]{0,2,1:T(8,128)(2,1)S(1)} %copy-done), kind=kOutput, calls=%fused_computation.6 | convolution fusion | flops 1512568832 | bytes 8347648 | tf_op jit(solution)/shard_map/gonv,gmv->gnom/dot_general | solution.py:25
  57.5 0.9 fusion.5
  58.4 0.7 copy-done.1
  59.1 3.5 %fusion.6 = (f32[128,16]{0,1:T(8,128)S(1)}, bf16[512,16,128]{2,0,1:T(8,128)(2,1)}) fusion(bf16[128,16,512]{0,2,1:T(8,128)(2,1)S(1)} %copy-done.1, f32[16,128]{1,0:T(8,128)S(1)} %fusion.5, f32[16,128]{1,0:T(8,128)S(1)} %get-tuple-element.14, f32[640,128,16]{1,0,2:T(8,128)S(1)} %get-tuple-element.15, bf16[1,640,576]{2,1,0:T(8,128)(2,1)S(1)} %bitcast.125), kind=kOutput, calls=%fused_computation.11 | convolution fusion | flops 1352660992 | bytes 10117120 | tf_op jit(solution)/shard_map/bhtk,bkl->bthl/dot_general | solution.py:32
  62.6 2.0 %fusion.7 = bf16[16,128,640]{1,2,0:T(8,128)(2,1)S(1)} fusion(f32[16,128]{1,0:T(8,128)S(1)} %bitcast.130, f32[16,128]{1,0:T(8,128)S(1)} %fusion.5, f32[16,128]{1,0:T(8,128)S(1)} %get-tuple-element.14, f32[640,128,16]{1,0,2:T(8,128)S(1)} %get-tuple-element.15, bf16[128,16,512]{0,2,1:T(8,128)(2,1)S(1)} %copy-done.1, bf16[1,640,576]{2,1,0:T(8,128)(2,1)S(1)} %bitcast.126), kind=kOutput, calls=%fused_computation.12 | convolution fusion | flops 1351352320 | bytes 10641408 | tf_op jit(solution)/shard_map/bthl,bkl->bhtk/dot_general | solution.py:36
  64.6 2.0 %convolution_bitcast_fusion = f32[1,640,576]{1,2,0:T(8,128)S(1)} fusion(bf16[16,128,640]{1,2,0:T(8,128)(2,1)S(1)} %fusion.7, bf16[128,16,576]{0,2,1:T(8,128)(2,1)S(1)} %copy-done), kind=kOutput, calls=%fused_computation.21 | convolution fusion | flops 1509949440 | bytes 6455296 | tf_op jit(solution)/shard_map/jxnq,jnxa->jqa/dot_general | solution.py:45
  66.6 1.9 %fusion.19 = f32[1,640,512]{1,2,0:T(8,128)S(1)} fusion(bf16[128,16,512]{0,2,1:T(8,128)(2,1)S(1)} %copy-done.1, f32[1,640,576]{1,2,0:T(8,128)S(1)} %convolution_bitcast_fusion, f32[16,128]{1,0:T(8,128)S(1)} %fusion.5, f32[16,128]{1,0:T(8,128)S(1)} %get-tuple-element.14, f32[640,128,16]{1,0,2:T(8,128)S(1)} %get-tuple-element.15), kind=kOutput, calls=%fused_computation.23 | convolution fusion | flops 1347747840 | bytes 9977856 | tf_op jit(solution)/shard_map/bhtk,bthl->bkl/dot_general | solution.py:48
  68.6 1.2 pad_maximum_fusion
  69.8 3.0 %copy.43 = f32[1,640,576]{2,1,0:T(8,128)} copy(f32[1,640,576]{1,2,0:T(8,128)} %pad_maximum_fusion) | data formatting | bytes 2949120 | tf_op jit(solution)/shard_map/concatenate | solution.py:51
  72.8 44.1 %all-reduce.2.cloned.1.call-done = f32[5,128,576]{2,1,0:T(8,128)} async-done(((f32[5,128,576]{2,1,0:T(8,128)}), f32[5,128,576]{2,1,0:T(8,128)}) %all-reduce.2.cloned.1.call-update) | async-done | bytes 1474576 | tf_op jit(solution)/shard_map/psum | solution.py:55
  117.0 1.0 constant_dynamic-slice_fusion
  118.0 0.2 reshape.186
  118.4 0.7 convolution_bitcast_fusion.1
  119.1 1.0 copy.45
  120.0 5.5 %all-to-all-start = ((f32[1,8,32,576]{3,2,0,1:T(8,128)}), f32[1,8,32,576]{3,2,0,1:T(8,128)S(1)}, u32[]{:S(2)}, u32[]{:S(2)}) async-start(f32[1,8,32,576]{3,2,0,1:T(8,128)} %copy.45), calls=%async_computation | async-start | bytes 1310720 | tf_op jit(solution)/shard_map/all_to_all | solution.py:71
  125.5 4.5 %copy.46 = bf16[128,16,512]{2,1,0:T(8,128)(2,1)} copy(bf16[128,16,512]{0,2,1:T(8,128)(2,1)} %bitcast.123) | data formatting | bytes 4194304
  130.1 5.4 %convert_bitcast_fusion = bf16[128,16,576]{0,2,1:T(8,128)(2,1)} fusion(bf16[640,576,1]{1,0,2:T(8,128)(2,1)} %bitcast.127, bf16[16,128,640]{1,2,0:T(8,128)(2,1)} %copy-done.3), kind=kOutput, calls=%fused_computation.18 | convolution fusion | flops 1511129088 | bytes 5718016 | tf_op jit(solution)/shard_map/mfgv,mvq->mgfq/dot_general | solution.py:42
  135.5 7.2 %all-to-all-done = f32[1,8,32,576]{3,2,0,1:T(8,128)S(1)} async-done(((f32[1,8,32,576]{3,2,0,1:T(8,128)}), f32[1,8,32,576]{3,2,0,1:T(8,128)S(1)}, u32[]{:S(2)}, u32[]{:S(2)}) %all-to-all-start) | async-done | bytes 589856 | tf_op jit(solution)/shard_map/all_to_all | solution.py:71
  142.7 0.7 reduce_sum.34
  (14 shorter events, 0.4 us)
Async XLA Ops:
  7.2 48.1 %copy-start = (bf16[128,16,576]{0,2,1:T(8,128)(2,1)S(1)}, bf16[128,16,576]{0,2,1:T(8,128)(2,1)}, u32[]{:S(2)}) copy-start(bf16[128,16,576]{0,2,1:T(8,128)(2,1)} %param.4) | copy-start | bytes 7077892
  7.2 109.8 %all-reduce.2.cloned.1.call-start = ((), (), s32[]{:S(2)}) async-start(), calls=%async_computation.1 | async-start | bytes 3276800 | tf_op jit(solution)/shard_map/psum | solution.py:55
  50.5 12.1 %copy-start.2 = (bf16[5,128,576]{2,1,0:T(8,128)(2,1)}, bf16[5,128,576]{2,1,0:T(8,128)(2,1)S(1)}, u32[]{:S(2)}) copy-start(bf16[5,128,576]{2,1,0:T(8,128)(2,1)S(1)} %all_gather.7) | copy-start | bytes 2211844
  57.5 1.6 %copy-start.1 = (bf16[128,16,512]{0,2,1:T(8,128)(2,1)S(1)}, bf16[128,16,512]{0,2,1:T(8,128)(2,1)}, u32[]{:S(2)}) copy-start(bf16[128,16,512]{0,2,1:T(8,128)(2,1)} %copy.37) | copy-start | bytes 6291460
  64.6 2.0 %copy-start.3 = (bf16[16,128,640]{1,2,0:T(8,128)(2,1)}, bf16[16,128,640]{1,2,0:T(8,128)(2,1)S(1)}, u32[]{:S(2)}) copy-start(bf16[16,128,640]{1,2,0:T(8,128)(2,1)S(1)} %fusion.7) | copy-start | bytes 7864324
  120.0 22.7 %all-to-all-start = ((f32[1,8,32,576]{3,2,0,1:T(8,128)}), f32[1,8,32,576]{3,2,0,1:T(8,128)S(1)}, u32[]{:S(2)}, u32[]{:S(2)}) async-start(f32[1,8,32,576]{3,2,0,1:T(8,128)} %copy.45), calls=%async_computation | async-start | bytes 1310720 | tf_op jit(solution)/shard_map/all_to_all | solution.py:71
Sparse Core Ops, SparseCore 0:
  73.0 43.9 all-reduce.1
where the time goes:
time: 151 us; the launch traced here: 150 us
  waiting for transfers between devices  51.3 us (34%)
  blocking collectives  41.7 us (28%)
  matrix products  17.7 us (12%)
  local copies, waits for them, and re-layouts  16.1 us (11%)
  between operations  14.1 us (9%)
  starting transfers between devices  5.55 us (4%)
  other arithmetic  3.74 us (2%)
    psum x1, waiting for transfers between devices, shards(): head_total = lax.psum(contrib, 'heads')  44.1 us
    all_gather x1, blocking collectives, shards(): slices = lax.all_gather(latents, 'seq', axis=0, tiled=True)  32.9 us
    unnamed x10, local copies, waits for them, and re-layouts  10 us
    all_gather x1, blocking collectives, shards(): key_row_tiles = lax.all_gather(picked, 'heads', axis=1, tiled=True)  8.8 us
    all_to_all x1, waiting for transfers between devices, shards(): lax.all_to_all(bundles, 'seq', split_axis=1, concat_axis=0, tiled=True)  7.21 us
    all_to_all x1, starting transfers between devices, shards(): lax.all_to_all(bundles, 'seq', split_axis=1, concat_axis=0, tiled=True)  5.51 us
    dot_general x1, matrix products, shards(): jnp.einsum('mfgv,mvq->mgfq', score_gradient, key_row_tiles, preferred_ele...  5.43 us
    dot_general x1, matrix products, shards(): jnp.einsum('bhtk,bkl->bthl', prob_half, value_rows, preferred_element_typ...  3.47 us
  transfers between devices with their start and end apart: 2, of which 2 were waited for; matrix products, arithmetic and copies ran while one was open for 7% of the time, Pallas kernels for 0%

commit v1 on v0

--- a/solution.py
+++ b/solution.py
@@ -52,7 +52,7 @@
         [key_gradient[:, :, :value_width] + grad_value, key_gradient[:, :, value_width:]], axis=-1
     )
     contrib = key_gradient.reshape(block_count * key_blocks, block_size, key_width)
-    head_total = lax.psum(contrib, "heads")
+    head_total = jnp.sum(lax.all_gather(contrib, "heads"), axis=0)
     own_share = lax.dynamic_slice_in_dim(
         head_total, lax.axis_index("heads") * row_share, row_share, 1
     )

time: 151 us -> 163 us (1.079)
  local copies, waits for them, and re-layouts: 16.1 us -> 23 us
  other arithmetic: 3.74 us -> 8.02 us
    all_gather x0 -> x1, waiting for transfers between devices: none -> 44.3 us  [shards(): head_total = jnp.sum(lax.all_gather(contrib, 'heads'), axis=0)]
    psum x1 -> x0, waiting for transfers between devices: 44.1 us -> none  [shards(): head_total = lax.psum(contrib, 'heads')]
    reduce_sum x0 -> x1, other arithmetic: none -> 4.26 us  [shards(): head_total = jnp.sum(lax.all_gather(contrib, 'heads'), axis=0)]
    dynamic_slice x1 -> x2, local copies, waits for them, and re-layouts: 1.03 us -> 4.79 us  [shards(): lax.dynamic_slice_in_dim(head_total, lax.axis_index('heads') * row_share,...]
    another operation x0 -> x1, local copies, waits for them, and re-layouts: none -> 3.11 us  [shards(): head_total = jnp.sum(lax.all_gather(contrib, 'heads'), axis=0)]
  transfers between devices with their start and end apart: 2 -> 2, of which waited for: 2 -> 2; matrix products, arithmetic and copies ran while one was open for 7% -> 6% of each run, Pallas kernels for 0% -> 0%
where the time goes in v1:
time: 163 us; the launch traced here: 162 us
  waiting for transfers between devices  52.1 us (32%)
  blocking collectives  41.7 us (26%)
  local copies, waits for them, and re-layouts  23 us (14%)
  matrix products  17.9 us (11%)
  between operations  14.1 us (9%)
  other arithmetic  8.02 us (5%)
  starting transfers between devices  5.55 us (3%)
    all_gather x1, waiting for transfers between devices, shards(): head_total = jnp.sum(lax.all_gather(contrib, 'heads'), axis=0)  44.3 us
    all_gather x1, blocking collectives, shards(): slices = lax.all_gather(latents, 'seq', axis=0, tiled=True)  32.9 us
    unnamed x10, local copies, waits for them, and re-layouts  10 us
    all_gather x1, blocking collectives, shards(): key_row_tiles = lax.all_gather(picked, 'heads', axis=1, tiled=True)  8.8 us
    all_to_all x1, waiting for transfers between devices, shards(): lax.all_to_all(bundles, 'seq', split_axis=1, concat_axis=0, tiled=True)  7.77 us
    all_to_all x1, starting transfers between devices, shards(): lax.all_to_all(bundles, 'seq', split_axis=1, concat_axis=0, tiled=True)  5.51 us
    dot_general x1, matrix products, shards(): jnp.einsum('mfgv,mvq->mgfq', score_gradient, key_row_tiles, preferred_ele...  5.43 us
    dynamic_slice x2, local copies, waits for them, and re-layouts, shards(): lax.dynamic_slice_in_dim(head_total, lax.axis_index('heads') * row_share,...  4.79 us
  transfers between devices with their start and end apart: 2, of which 2 were waited for; matrix products, arithmetic and copies ran while one was open for 6% of the time, Pallas kernels for 0%

profile of v1, /device:TPU:0, one launch (start us, length us, event | category | flops | bytes accessed | tf_op | source)
XLA Modules:
  0.0 162.4 jit_solution(16008847229562464408)
XLA Ops:
  7.2 0.9 compare_and_fusion
  8.1 32.9 %all_gather.9 = bf16[8,32,576]{2,1,0:T(8,128)(2,1)S(1)} all-gather(bf16[1,32,576]{2,1,0:T(8,128)(2,1)} %param.5), channel_id=1, replica_groups=mesh['heads'=4,'seq'=8] {'seq'}, dimensions={0}, use_global_device_ids=true | all-gather | bytes 331776 | tf_op jit(solution)/shard_map/all_gather | solution.py:14
  41.7 8.8 %all_gather.10 = bf16[5,128,576]{2,1,0:T(8,128)(2,1)S(1)} all-gather(bf16[5,32,576]{2,1,0:T(8,128)(2,1)S(1)} %broadcast_select_fusion), channel_id=1, replica_groups=mesh['heads'=4,'seq'=8] {'heads'}, dimensions={1}, use_global_device_ids=true | all-gather | bytes 921600 | tf_op jit(solution)/shard_map/all_gather | solution.py:19
  50.5 4.8 %copy.69 = bf16[128,16,512]{0,2,1:T(8,128)(2,1)} copy(bf16[128,16,512]{2,1,0:T(8,128)(2,1)} %param.6) | data formatting | bytes 4194304 | tf_op args[2]
  55.3 2.2 %bitcast_reduce_fusion = (f32[16,128]{1,0:T(8,128)S(1)}, f32[640,128,16]{1,0,2:T(8,128)S(1)}) fusion(bf16[640,576,1]{1,0,2:T(8,128)(2,1)S(1)} %bitcast.124, bf16[128,16,576]{0,2,1:T(8,128)(2,1)S(1)} %copy-done), kind=kOutput, calls=%fused_computation.6 | convolution fusion | flops 1512568832 | bytes 8347648 | tf_op jit(solution)/shard_map/gonv,gmv->gnom/dot_general | solution.py:25
  57.5 0.9 fusion.5
  58.4 0.7 copy-done.1
  59.1 3.5 %fusion.6 = (f32[128,16]{0,1:T(8,128)S(1)}, bf16[512,16,128]{2,0,1:T(8,128)(2,1)}) fusion(bf16[128,16,512]{0,2,1:T(8,128)(2,1)S(1)} %copy-done.1, f32[16,128]{1,0:T(8,128)S(1)} %fusion.5, f32[16,128]{1,0:T(8,128)S(1)} %get-tuple-element.20, f32[640,128,16]{1,0,2:T(8,128)S(1)} %get-tuple-element.21, bf16[1,640,576]{2,1,0:T(8,128)(2,1)S(1)} %bitcast.125), kind=kOutput, calls=%fused_computation.11 | convolution fusion | flops 1352660992 | bytes 10117120 | tf_op jit(solution)/shard_map/bhtk,bkl->bthl/dot_general | solution.py:32
  62.6 2.2 %fusion.7 = bf16[16,128,640]{1,2,0:T(8,128)(2,1)S(1)} fusion(f32[16,128]{1,0:T(8,128)S(1)} %bitcast.130, f32[16,128]{1,0:T(8,128)S(1)} %fusion.5, f32[16,128]{1,0:T(8,128)S(1)} %get-tuple-element.20, f32[640,128,16]{1,0,2:T(8,128)S(1)} %get-tuple-element.21, bf16[128,16,512]{0,2,1:T(8,128)(2,1)S(1)} %copy-done.1, bf16[1,640,576]{2,1,0:T(8,128)(2,1)S(1)} %bitcast.126), kind=kOutput, calls=%fused_computation.12 | convolution fusion | flops 1351352320 | bytes 10641408 | tf_op jit(solution)/shard_map/bthl,bkl->bhtk/dot_general | solution.py:36
  64.8 2.0 %convolution_bitcast_fusion = f32[1,640,576]{1,2,0:T(8,128)S(1)} fusion(bf16[16,128,640]{1,2,0:T(8,128)(2,1)S(1)} %fusion.7, bf16[128,16,576]{0,2,1:T(8,128)(2,1)S(1)} %copy-done), kind=kOutput, calls=%fused_computation.21 | convolution fusion | flops 1509949440 | bytes 6455296 | tf_op jit(solution)/shard_map/jxnq,jnxa->jqa/dot_general | solution.py:45
  66.8 1.9 %fusion.19 = f32[1,640,512]{1,2,0:T(8,128)S(1)} fusion(bf16[128,16,512]{0,2,1:T(8,128)(2,1)S(1)} %copy-done.1, f32[1,640,576]{1,2,0:T(8,128)S(1)} %convolution_bitcast_fusion, f32[16,128]{1,0:T(8,128)S(1)} %fusion.5, f32[16,128]{1,0:T(8,128)S(1)} %get-tuple-element.20, f32[640,128,16]{1,0,2:T(8,128)S(1)} %get-tuple-element.21), kind=kOutput, calls=%fused_computation.23 | convolution fusion | flops 1347747840 | bytes 9977856 | tf_op jit(solution)/shard_map/bhtk,bthl->bkl/dot_general | solution.py:48
  68.7 1.2 pad_maximum_fusion
  70.0 3.0 %copy.75 = f32[1,640,576]{2,1,0:T(8,128)} copy(f32[1,640,576]{1,2,0:T(8,128)} %pad_maximum_fusion) | data formatting | bytes 2949120 | tf_op jit(solution)/shard_map/concatenate | solution.py:51
  73.0 3.1 %copy.76 = f32[1,5,128,576]{2,3,1,0:T(8,128)} copy(f32[1,5,128,576]{3,2,1,0:T(8,128)} %bitcast.121) | data formatting | bytes 2949120 | tf_op jit(solution)/shard_map/all_gather;reshape | solution.py:55
  76.1 44.3 %all-gather.2.cloned.1.call-done = f32[4,5,128,576]{2,3,1,0:T(8,128)} async-done(((f32[1,5,128,576]{2,3,1,0:T(8,128)}), f32[4,5,128,576]{2,3,1,0:T(8,128)}) %all-gather.2.cloned.1.call-update) | async-done | bytes 5898256 | tf_op jit(solution)/shard_map/all_gather | solution.py:55
  120.5 4.3 %reduce_sum.43 = f32[5,128,576]{1,2,0:T(8,128)} reduce(f32[4,5,128,576]{2,3,1,0:T(8,128)} %all-gather.2.cloned.1.call-done, f32[]{:T(128)} %constant.32.clone.1), dimensions={0}, to_apply=%region_3.4 | reduce | flops 1105920 | bytes 7372804 | tf_op jit(solution)/shard_map/reduce_sum | solution.py:55
  124.7 3.0 %constant_dynamic-slice_fusion = f32[5,32,576]{1,2,0:T(8,128)} fusion(f32[5,128,576]{1,2,0:T(8,128)} %reduce_sum.43, s32[]{:T(128)S(6)} %select_n.26), kind=kLoop, calls=%fused_computation.37 | loop fusion | bytes 737284 | tf_op jit(solution)/shard_map/dynamic_slice | solution.py:56
  127.7 1.8 %copy.77 = f32[5,32,576]{2,1,0:T(8,128)S(1)} copy(f32[5,32,576]{1,2,0:T(8,128)} %constant_dynamic-slice_fusion) | data formatting | bytes 737280 | tf_op jit(solution)/shard_map/dynamic_slice | solution.py:56
  130.6 1.0 copy.79
  131.6 5.5 %all-to-all-start = ((f32[1,8,32,576]{3,2,0,1:T(8,128)}), f32[1,8,32,576]{3,2,0,1:T(8,128)S(1)}, u32[]{:S(2)}, u32[]{:S(2)}) async-start(f32[1,8,32,576]{3,2,0,1:T(8,128)} %copy.79), calls=%async_computation | async-start | bytes 1310720 | tf_op jit(solution)/shard_map/all_to_all | solution.py:71
  137.1 4.5 %copy.80 = bf16[128,16,512]{2,1,0:T(8,128)(2,1)} copy(bf16[128,16,512]{0,2,1:T(8,128)(2,1)} %bitcast.123) | data formatting | bytes 4194304
  141.6 5.4 %convert_bitcast_fusion = bf16[128,16,576]{0,2,1:T(8,128)(2,1)} fusion(bf16[640,576,1]{1,0,2:T(8,128)(2,1)} %bitcast.127, bf16[16,128,640]{1,2,0:T(8,128)(2,1)} %copy-done.3), kind=kOutput, calls=%fused_computation.18 | convolution fusion | flops 1511129088 | bytes 5718016 | tf_op jit(solution)/shard_map/mfgv,mvq->mgfq/dot_general | solution.py:42
  147.1 7.8 %all-to-all-done = f32[1,8,32,576]{3,2,0,1:T(8,128)S(1)} async-done(((f32[1,8,32,576]{3,2,0,1:T(8,128)}), f32[1,8,32,576]{3,2,0,1:T(8,128)S(1)}, u32[]{:S(2)}, u32[]{:S(2)}) %all-to-all-start) | async-done | bytes 589856 | tf_op jit(solution)/shard_map/all_to_all | solution.py:71
  154.8 0.7 reduce_sum.44
  (17 shorter events, 1.9 us)
Async XLA Ops:
  7.2 48.1 %copy-start = (bf16[128,16,576]{0,2,1:T(8,128)(2,1)S(1)}, bf16[128,16,576]{0,2,1:T(8,128)(2,1)}, u32[]{:S(2)}) copy-start(bf16[128,16,576]{0,2,1:T(8,128)(2,1)} %param.4) | copy-start | bytes 7077892
  7.2 113.3 %all-gather.2.cloned.1.call-start = ((), (), s32[]{:S(2)}) async-start(), calls=%async_computation.1 | async-start | bytes 7372800 | tf_op jit(solution)/shard_map/all_gather | solution.py:55
  50.5 12.1 %copy-start.2 = (bf16[5,128,576]{2,1,0:T(8,128)(2,1)}, bf16[5,128,576]{2,1,0:T(8,128)(2,1)S(1)}, u32[]{:S(2)}) copy-start(bf16[5,128,576]{2,1,0:T(8,128)(2,1)S(1)} %all_gather.10) | copy-start | bytes 2211844
  57.5 1.6 copy-start.1
  64.8 2.0 %copy-start.3 = (bf16[16,128,640]{1,2,0:T(8,128)(2,1)}, bf16[16,128,640]{1,2,0:T(8,128)(2,1)S(1)}, u32[]{:S(2)}) copy-start(bf16[16,128,640]{1,2,0:T(8,128)(2,1)S(1)} %fusion.7) | copy-start | bytes 7864324
  131.6 23.2 %all-to-all-start = ((f32[1,8,32,576]{3,2,0,1:T(8,128)}), f32[1,8,32,576]{3,2,0,1:T(8,128)S(1)}, u32[]{:S(2)}, u32[]{:S(2)}) async-start(f32[1,8,32,576]{3,2,0,1:T(8,128)} %copy.79), calls=%async_computation | async-start | bytes 1310720 | tf_op jit(solution)/shard_map/all_to_all | solution.py:71
Sparse Core Ops, SparseCore 0:
  76.3 44.1 all-gather.1
